TPU v7x, 128 devices: a whole 4x4x4 slice. The times are simulated.
128 devices in a mesh: member: 8 (over z, y_lo), space: 16 (over x, y_hi, core).
Axes of the slice: x: 4, y: 4 (y_hi: 2, y_lo: 2; y = y_hi * 2 + y_lo), z: 4, core: 2. Of those that a mesh axis runs over, the one named last changes fastest.
Arguments:
- features: bfloat16 [8, 1024, 65536], P('member', None, 'space'), may hold values from -6 to 6
- up_weight: bfloat16 [1024, 1024], replicated, may hold values from -0.1875 to 0.1875
- out_weight: bfloat16 [1024, 100], replicated, may hold values from -0.1875 to 0.1875
- target: bfloat16 [100, 65536], P(None, 'space'), may hold values from -6 to 6
- area: float32 [65536], P('space'), may hold values from 0.1 to 1
Outputs:
- feature_grad: bfloat16 [8, 1024, 65536], P('member', None, 'space')
- up_grad: float32 [1024, 1024], P(('member', 'space'))
- out_grad: float32 [1024, 100], P(('member', 'space'))
All inputs are finite; a program needn't handle non-finite values.
Results may differ from a plain program's by a relative error of at most 0.007.
Values sent between devices are 32-bit elements; how exact they have to be, the bound alone decides.
No kernel may reach another device: no remote copies, remote signals or barrier semaphores. Data moves between devices by JAX's collectives and lax.ppermute only.
A program may use at most 128 MiB of HBM per device.

v0:
```python
import functools
import math

import jax
import jax.numpy as jnp
from jax import lax
from jax.experimental import pallas as pl
from jax.experimental.pallas import tpu as pltpu
from jax.sharding import Mesh
from jax.sharding import PartitionSpec as P


MEMBER = ("z", "ylo")
CHIP = ("z", "ylo", "x", "yhi")
SPACE = ("x", "yhi", "core")
DEVICE = ("z", "ylo", "x", "yhi", "core")

NEAR = ((1, 0), (3, 0), (1, 1), (3, 1))
SIDE = ((0, 0), (0, 1))
FAR = ((2, 0), (2, 1))
SLOTS = NEAR + SIDE + FAR
FIRST = ((2, 1), (2, 0), (1, 1), (3, 1), (0, 1))
SECOND = ((1, 0), (3, 0), (0, 0))
ORDER = FIRST + SECOND

TILE = 512
SPAN = 1024
BLOCK = 512
HALF = 256
ROWS = 256
MIB = 1 << 20
BF16, F32 = jnp.bfloat16, jnp.float32


def route(slot, back):
    pairs = []
    for z in range(4):
        for y in range(2):
            here, there = 2 * z + y, 2 * ((z + slot[0]) % 4) + (y ^ slot[1])
            pairs.append((there, here) if back else (here, there))
    return pairs


def in_hbm(x):
    return pltpu.with_memory_space_constraint(x, pltpu.HBM)


def in_vmem(x):
    return pltpu.with_memory_space_constraint(x, pltpu.VMEM)


def smooth(diff):
    return diff * lax.rsqrt(diff * diff + 0.0625)


def mm(a, b, ca, cb):
    return lax.dot_general(a, b, (((ca,), (cb,)), ((), ())), preferred_element_type=F32)


def forward_kernel(first, info, *refs):
    if first:
        x, w, owt, hidden, slope, *preds, wt, ow = refs
    else:
        x, wt, owt, _, _, hidden, slope, *preds = refs
    step = pl.program_id(0)

    if first:

        @pl.when(step == 0)
        def _():
            for i in range(0, w.shape[0], ROWS):
                wt[:, i : i + ROWS] = (w[i : i + ROWS, :] * 0.5).T
            ow[...] = (owt[...] * 0.5).T

    slot = info[17 + (0 if first else len(FIRST)) + step]
    h = mm(wt[...], x[...], 1, 0)
    u = jnp.tanh(h) + 1.0
    act = h * u
    rounded = act.astype(BF16)
    hidden[slot] = rounded
    slope[slot] = (u + act * (2.0 - u)).astype(BF16)
    pred = mm(owt[...], rounded, 1, 0)
    for i, out in enumerate(preds):

        @pl.when(step == i)
        def _():
            out[...] = pred


def forward(info, x, w, owt, carried=None):
    first = carried is None
    depth, _ = x.shape
    channels = owt.shape[0]
    n, base = (len(FIRST), 0) if first else (len(SECOND), len(FIRST))
    at_tile = pl.BlockSpec((depth, TILE), lambda g, t: (0, t[9 + base + g]))
    whole = lambda *s: pl.BlockSpec(s, lambda g, t: (0,) * len(s))
    fixed = pl.BlockSpec(memory_space=pltpu.VMEM)
    act = pltpu.VMEM((len(SLOTS), depth, TILE), BF16)
    out_shape = [act, act] + [pltpu.VMEM((channels, TILE), F32)] * n
    out_specs = [fixed, fixed] + [fixed] * n
    w_spec = whole(depth, depth) if first else fixed
    w = in_hbm(w) if first else in_vmem(w)
    args, in_specs = [in_hbm(x), w, in_hbm(owt)], [at_tile, w_spec, whole(channels, depth)]
    alias = {}
    if first:
        out_shape += [pltpu.VMEM((depth, depth), BF16), pltpu.HBM((depth, channels), BF16)]
        out_specs += [fixed, whole(depth, channels)]
    else:
        out_shape[-1] = pltpu.HBM((channels, TILE), F32)
        out_specs[-1] = whole(channels, TILE)
        args += map(in_vmem, carried)
        in_specs += [fixed, fixed]
        alias = {4: 0, 5: 1}
    return pl.pallas_call(
        functools.partial(forward_kernel, first),
        grid_spec=pltpu.PrefetchScalarGridSpec(
            num_scalar_prefetch=1, grid=(n,), in_specs=in_specs, out_specs=out_specs
        ),
        out_shape=out_shape,
        input_output_aliases=alias,
        compiler_params=pltpu.CompilerParams(vmem_limit_bytes=16 * MIB),
        cost_estimate=pl.CostEstimate(
            flops=2 * depth * (depth + channels) * TILE * n,
            bytes_accessed=6 * depth * TILE * n + 2 * depth * depth,
            transcendentals=depth * TILE * n,
        ),
        name="forward",
    )(info, *args)


def pair_kernel(info, *refs):
    preds, (target, area), outs = refs[:8], refs[8:10], refs[10:]
    own_out, side_out, *near_outs = outs
    members = len(SLOTS)
    across = 0.95 / (members * (members - 1))
    channels = target.shape[0]
    for lane in range(0, TILE, 128):
        cols = slice(lane, lane + 128)
        weight = area[:, cols]
        second = lane >= HALF
        at = lane % HALF
        tail = slice(TILE + at, TILE + at + 128)
        for low in range(0, channels, 8):
            rows = slice(low, min(low + 8, channels))
            p = [r[rows, cols] for r in preds]
            t = target[rows, cols].astype(F32)
            total = [None] * members
            for a in range(members):
                for b in range(a + 1, members):
                    s = smooth(p[a] - p[b])
                    total[a] = s if total[a] is None else total[a] + s
                    total[b] = -s if total[b] is None else total[b] - s
            for a in range(members):
                g = weight * (smooth(p[a] - t) * (1.0 / members) - across * total[a])
                g = g.astype(BF16).astype(F32)
                if a < 6:
                    outs[a][rows, cols] = g
                else:
                    near_outs[2 * (a - 6) + second][rows, tail] = g


def pairs(info, preds, target, area):
    channels = target.shape[0]
    me = 1 + SLOTS.index((0, 0))
    fixed = pl.BlockSpec(memory_space=pltpu.VMEM)
    whole = pl.BlockSpec((channels, TILE), lambda g, t: (0, 0))
    return pl.pallas_call(
        pair_kernel,
        grid_spec=pltpu.PrefetchScalarGridSpec(
            num_scalar_prefetch=1,
            grid=(1,),
            in_specs=[whole]
            + [fixed] * 7
            + [
                pl.BlockSpec((channels, TILE), lambda g, t: (0, t[me])),
                pl.BlockSpec((1, TILE), lambda g, t: (0, t[me])),
            ],
            out_specs=[whole] + [fixed] * 5,
        ),
        out_shape=[pltpu.HBM((channels, TILE), F32), pltpu.VMEM((channels, TILE), F32)]
        + [pltpu.VMEM((channels, TILE + HALF), F32)] * 4,
        compiler_params=pltpu.CompilerParams(vmem_limit_bytes=16 * MIB),
        cost_estimate=pl.CostEstimate(
            flops=36 * 6 * channels * TILE,
            bytes_accessed=64 * channels * TILE,
            transcendentals=36 * channels * TILE,
        ),
        name="pairs",
    )(info, in_hbm(preds[0]), *map(in_vmem, preds[1:]), target, area)


def join_kernel(left, right, out):
    out[:, :HALF] = left[:, TILE:]
    out[:, HALF:] = right[:, TILE:]


def join_tails(left, right):
    fixed = pl.BlockSpec(memory_space=pltpu.VMEM)
    return pl.pallas_call(
        join_kernel,
        in_specs=[fixed, fixed],
        out_specs=fixed,
        out_shape=pltpu.VMEM((left.shape[0], 2 * HALF), F32),
        compiler_params=pltpu.CompilerParams(vmem_limit_bytes=4 * MIB),
        name="join_tails",
    )(in_vmem(left), in_vmem(right))


def backward_kernel(info, *refs):
    near, own, side, relayed = refs[:4], refs[4], refs[5], refs[6:8]
    x_hbm, hidden, slope, ow, grad, away, keep, pg, x, up, out, sem = refs[8:]
    block, chunk = pl.program_id(0), pl.program_id(1)
    channels, each = pg.shape[0], grad.shape[0]
    wide, chunks = each * TILE, len(SLOTS) // each

    def fetch(i):
        tile = pl.ds(pl.multiple_of(info[1 + i] * TILE, TILE), TILE)
        place = slice(i * TILE, (i + 1) * TILE)
        return pltpu.make_async_copy(x_hbm.at[:, tile], x.at[:, place], sem.at[i])

    @pl.when((block == 0) & (chunk == 0))
    def _():
        for i in range(len(SLOTS)):
            fetch(i).start()
        for i, ref in enumerate((*near, own, side)):
            pg[:, i * TILE : (i + 1) * TILE] = ref[:, :TILE].astype(BF16)
        for i in range(len(FAR)):
            for k, ref in enumerate(relayed):
                low = (6 + i) * TILE + k * HALF
                pg[:, low : low + HALF] = ref[:, i * HALF : (i + 1) * HALF].astype(BF16)

    for c in range(chunks):

        @pl.when((block == 0) & (chunk == c))
        def _():
            for i in range(c * each, (c + 1) * each):
                fetch(i).wait()

    span = pl.ds(pl.multiple_of(chunk * wide, wide), wide)
    pgt = pg[:, span]
    own_rows = pl.ds(pl.multiple_of(block * BLOCK, BLOCK), BLOCK)
    for low in range(0, wide, ROWS):
        hg = mm(ow[...], pgt[:, low : low + ROWS], 1, 0)
        i, cols = low // TILE, slice(low % TILE, low % TILE + ROWS)
        factor = slope[chunk * each + i, own_rows, cols]
        grad[i, :, cols] = (hg * factor.astype(F32)).astype(BF16)
    acts = [hidden[chunk * each + i, own_rows, :] for i in range(each)]
    joined = jnp.concatenate([grad[i] for i in range(each)], axis=1)
    opening = chunk == 0
    part_out = mm(pgt, jnp.concatenate(acts, axis=1), 1, 1)
    out[:channels, :] = jnp.where(opening, 0.0, out[:channels, :]) + part_out
    part_up = mm(x[:, span], joined, 1, 1).reshape(up.shape)
    up[...] = jnp.where(opening, 0.0, up[...]) + part_up

    @pl.when(chunk == chunks - 1)
    def _():
        depth = keep.shape[2] - 128
        cols = pl.ds(pl.multiple_of(block * BLOCK, BLOCK), BLOCK)
        some = BLOCK // 16
        rows = pl.ds(block * some, some)
        for ref, core in ((keep, info[0]), (away, 1 - info[0])):
            ref[:, :, cols] = up[:, core]
        up[:some, :, :, :128] = out[...].T.reshape(some, 2, 8, 128)
        for ref, core in ((keep, info[0]), (away, 1 - info[0])):
            ref[rows, :, depth:] = up[:some, core, :, :128]


def backward(info, near, own, side, relayed, x, hidden, slope, ow):
    depth, cells = x.shape
    channels = ow.shape[1]
    chips, blocks = depth // 16, depth // BLOCK
    at = pl.BlockSpec((SPAN // TILE, BLOCK, TILE), lambda b, c, t: (c, b, 0))
    fixed = pl.BlockSpec(memory_space=pltpu.VMEM)
    return pl.pallas_call(
        backward_kernel,
        grid_spec=pltpu.PrefetchScalarGridSpec(
            num_scalar_prefetch=1,
            grid=(blocks, cells // SPAN),
            in_specs=[fixed] * 4
            + [pl.BlockSpec((channels, TILE), lambda b, c, t: (0, 0))]
            + [fixed] * 3
            + [
                pl.BlockSpec(memory_space=pl.ANY),
                fixed,
                fixed,
                pl.BlockSpec((BLOCK, channels), lambda b, c, t: (b, 0)),
            ],
            out_specs=[at, fixed, fixed],
            scratch_shapes=[
                pltpu.VMEM((channels, cells), BF16),
                pltpu.VMEM((depth, cells), BF16),
                pltpu.VMEM((chips, 2, 8, BLOCK), F32),
                pltpu.VMEM((128, BLOCK), F32),
                pltpu.SemaphoreType.DMA((len(SLOTS),)),
            ],
        ),
        out_shape=[pltpu.HBM(hidden.shape, BF16)]
        + [pltpu.VMEM((chips, 8, depth + 128), F32)] * 2,
        compiler_params=pltpu.CompilerParams(vmem_limit_bytes=28 * MIB),
        cost_estimate=pl.CostEstimate(
            flops=2 * depth * (depth + 2 * channels) * cells,
            bytes_accessed=8 * depth * cells + 4 * depth * depth,
            transcendentals=0,
        ),
        name="backward",
    )(
        info,
        *map(in_vmem, near),
        in_hbm(own),
        *map(in_vmem, (side, *relayed)),
        in_hbm(x),
        in_vmem(hidden),
        in_vmem(slope),
        in_hbm(ow),
    )


def feature_kernel(table, w, grad, out):
    out[0] = mm(w[...], grad[0], 1, 0).astype(BF16)


def feature_grad(table, w, grad):
    depth, cells = grad.shape[1], grad.shape[0] * TILE
    return pl.pallas_call(
        feature_kernel,
        grid_spec=pltpu.PrefetchScalarGridSpec(
            num_scalar_prefetch=1,
            grid=(cells // TILE,),
            in_specs=[
                pl.BlockSpec((depth, depth), lambda g, t: (0, 0)),
                pl.BlockSpec((1, depth, TILE), lambda g, t: (g, 0, 0)),
            ],
            out_specs=pl.BlockSpec((1, depth, TILE), lambda g, t: (0, 0, t[1 + g])),
        ),
        out_shape=jax.ShapeDtypeStruct((1, depth, cells), BF16),
        compiler_params=pltpu.CompilerParams(vmem_limit_bytes=24 * MIB),
        cost_estimate=pl.CostEstimate(
            flops=2 * depth * depth * cells,
            bytes_accessed=4 * depth * cells + 2 * depth * depth,
            transcendentals=0,
        ),
        name="feature_grad",
    )(table, in_hbm(w), in_hbm(grad))


def total_kernel(scale, parts, up, out):
    depth, channels = up.shape[1], out.shape[1]
    acc = parts[0]
    for c in range(1, parts.shape[0]):
        acc = acc + parts[c]
    acc = acc * scale
    up[...] = acc[:, :depth]
    out[...] = acc[:, depth : depth + channels]


def total(parts, depth, channels, scale):
    rows = parts.shape[1]
    return pl.pallas_call(
        functools.partial(total_kernel, scale),
        in_specs=[pl.BlockSpec(memory_space=pltpu.VMEM)],
        out_shape=[
            jax.ShapeDtypeStruct((rows, depth), F32),
            jax.ShapeDtypeStruct((rows, channels), F32),
        ],
        compiler_params=pltpu.CompilerParams(vmem_limit_bytes=16 * MIB),
        name="total",
    )(parts)


def spread(away, keep):
    swapped = lax.ppermute(away, "core", [(0, 1), (1, 0)])
    return lax.all_to_all(keep + swapped, CHIP, 0, 0, tiled=True)


def body(features, up_weight, out_weight, target, area):
    x = features[0]
    depth, cells = x.shape
    channels = out_weight.shape[1]
    owt = out_weight.T
    z, y = lax.axis_index("z"), lax.axis_index("ylo")
    core = lax.axis_index("core")

    tiles = {
        s: (2 * lax.rem(z + s[0], 4) + lax.bitwise_xor(y, s[1])).astype(jnp.int32) for s in SLOTS
    }
    info = [core.astype(jnp.int32)] + [tiles[s] for s in SLOTS + ORDER]
    info = jnp.stack(info + [jnp.int32(SLOTS.index(s)) for s in ORDER])

    def relay(blocks, step):
        return lax.ppermute(join_tails(*blocks), "z", [(i, (i + step) % 4) for i in range(4)])

    hidden, slope, *sent, wt, ow = forward(info, x, up_weight, owt)
    got = {}
    for s, p in zip(FIRST, sent):
        got[s] = lax.ppermute(p, MEMBER, route(s, False))
    hidden, slope, *sent = forward(info, x, wt, owt, (hidden, slope))
    for s, p in zip(SECOND, sent):
        got[s] = p if s == (0, 0) else lax.ppermute(p, MEMBER, route(s, False))
    order = SIDE + NEAR + FAR
    own, side, *sent = pairs(info, [got[s] for s in order], target, area[None, :])

    near = [lax.ppermute(block, MEMBER, route(s, True)) for s, block in zip(NEAR, sent)]
    side = lax.ppermute(side, MEMBER, route((0, 1), True))
    relayed = relay(near[0::2], -1), relay(near[1::2], 1)
    pre_grad, away, keep = backward(info, near, own, side, relayed, x, hidden, slope, ow)
    parts = spread(away, keep)
    fgrad = feature_grad(info, up_weight, pre_grad)
    scale = 1.0 / math.sqrt(cells * lax.axis_size(SPACE) * lax.axis_size(MEMBER))
    up_grad, out_grad = total(parts, depth, channels, scale)
    return fgrad, up_grad, out_grad


def solution(mesh):
    fine = Mesh(mesh.devices.reshape(4, 2, 4, 2, 2), DEVICE)
    in_specs = (P(MEMBER, None, SPACE), P(), P(), P(None, SPACE), P(SPACE))
    out_specs = (P(MEMBER, None, SPACE), P(DEVICE, None), P(DEVICE, None))
    return jax.shard_map(body, mesh=fine, in_specs=in_specs, out_specs=out_specs, check_vma=False)
```

profile of v0, /device:TPU:1, one launch (start us, length us, event | category | flops | bytes accessed | tf_op | source)
XLA Modules:
  0.0 145.8 jit_solution(5638464249491165293)
XLA Ops:
  0.8 13.0 %forward.2 = (bf16[8,1024,512]{2,1,0:T(8,128)(2,1)S(1)}, bf16[8,1024,512]{2,1,0:T(8,128)(2,1)S(1)}, f32[100,512]{1,0:T(8,128)S(1)}, f32[100,512]{1,0:T(8,128)S(1...) custom-call(s32[25]{0:T(128)S(1)} %stack.47.info.table, ...), custom_call_target="tpu_custom_call" | custom-call | flops 5892997120 | bytes 17825792 | tf_op jit(solution)/shard_map/forward/pallas_call | solution.py:114
  13.8 7.9 %forward.3 = (bf16[8,1024,512]{2,1,0:T(8,128)(2,1)S(1)}, bf16[8,1024,512]{2,1,0:T(8,128)(2,1)S(1)}, f32[100,512]{1,0:T(8,128)S(1)}, f32[100,512]{1,0:T(8,128)S(1)}, f32[100,512]{1,0:T(8,128)}) custom-call(s32[25]{0:T(128)S(1)} %stack.47.info.table, bf16[1024,4096]{1,0:T(8,128)(2,1)} %bitcast.14, ...), custom_call_target="tpu_custom_call", output_to_operand_aliasing={{0}: (4, {}), {1}: (5, {})} | custom-call | flops 3535798272 | bytes 11534336 | tf_op jit(solution)/shard_map/forward/pallas_call | solution.py:114
  21.7 2.5 %collective-permute-start.1 = (f32[100,512]{1,0:T(8,128)S(1)}, f32[100,512]{1,0:T(8,128)S(1)}, u32[]{:S(2)}, u32[]{:S(2)}) collective-permute-start(f32[100,512]{1,0:T(8,128)S(1)} %get-tuple-element.33), channel_id=1, source_target_pairs={{0,32},{16,48},{32,64},{48,80},{64,96},{80,112},{96,0},{112,16},{1... | collective-permute-start | bytes 614408 | tf_op jit(solution)/shard_map/ppermute | solution.py:398
  24.2 2.1 %collective-permute-start.2 = (f32[100,512]{1,0:T(8,128)S(1)}, f32[100,512]{1,0:T(8,128)S(1)}, u32[]{:S(2)}, u32[]{:S(2)}) collective-permute-start(f32[100,512]{1,0:T(8,128)S(1)} %get-tuple-element.34), channel_id=1, source_target_pairs={{0,96},{16,112},{32,0},{48,16},{64,32},{80,48},{96,64},{112,80},{1... | collective-permute-start | bytes 614408 | tf_op jit(solution)/shard_map/ppermute | solution.py:398
  27.6 3.6 %collective-permute-start.4 = (f32[100,512]{1,0:T(8,128)S(1)}, f32[100,512]{1,0:T(8,128)S(1)}, u32[]{:S(2)}, u32[]{:S(2)}) collective-permute-start(f32[100,512]{1,0:T(8,128)S(1)} %get-tuple-element.36), channel_id=1, source_target_pairs={{0,112},{16,96},{32,16},{48,0},{64,48},{80,32},{96,80},{112,64},{1... | collective-permute-start | bytes 614408 | tf_op jit(solution)/shard_map/ppermute | solution.py:395
  32.3 2.9 %collective-permute-start.6 = (f32[100,512]{1,0:T(8,128)S(1)}, f32[100,512]{1,0:T(8,128)S(1)}, u32[]{:S(2)}, u32[]{:S(2)}) collective-permute-start(f32[100,512]{1,0:T(8,128)S(1)} %get-tuple-element.38), channel_id=1, source_target_pairs={{0,80},{16,64},{32,112},{48,96},{64,16},{80,0},{96,48},{112,32},{1... | collective-permute-start | bytes 614408 | tf_op jit(solution)/shard_map/ppermute | solution.py:395
  35.2 2.4 %collective-permute-done.3.refs_4_ = f32[100,512]{1,0:T(8,128)S(1)} collective-permute-done((f32[100,512]{1,0:T(8,128)S(1)}, f32[100,512]{1,0:T(8,128)S(1)}, u32[]{:S(2)}, u32[]{:S(2)}) %collective-permute-start.3) | collective-permute-done | bytes 204832 | tf_op jit(solution)/shard_map/ppermute | solution.py:395
  37.6 2.9 %collective-permute-done.4.refs_5_ = f32[100,512]{1,0:T(8,128)S(1)} collective-permute-done((f32[100,512]{1,0:T(8,128)S(1)}, f32[100,512]{1,0:T(8,128)S(1)}, u32[]{:S(2)}, u32[]{:S(2)}) %collective-permute-start.4) | collective-permute-done | bytes 204832 | tf_op jit(solution)/shard_map/ppermute | solution.py:395
  40.5 2.9 %collective-permute-done.5.refs_6_ = f32[100,512]{1,0:T(8,128)S(1)} collective-permute-done((f32[100,512]{1,0:T(8,128)S(1)}, f32[100,512]{1,0:T(8,128)S(1)}, u32[]{:S(2)}, u32[]{:S(2)}) %collective-permute-start.5) | collective-permute-done | bytes 204832 | tf_op jit(solution)/shard_map/ppermute | solution.py:395
  43.4 3.4 %collective-permute-done.6.refs_7_ = f32[100,512]{1,0:T(8,128)S(1)} collective-permute-done((f32[100,512]{1,0:T(8,128)S(1)}, f32[100,512]{1,0:T(8,128)S(1)}, u32[]{:S(2)}, u32[]{:S(2)}) %collective-permute-start.6) | collective-permute-done | bytes 204832 | tf_op jit(solution)/shard_map/ppermute | solution.py:395
  46.8 3.4 %pairs.1 = (f32[100,512]{1,0:T(8,128)}, f32[100,512]{1,0:T(8,128)S(1)}, f32[100,768]{1,0:T(8,128)S(1)}, f32[100,768]{1,0:T(8,128)S(1)}, f32[100,768]{1,0:T(8,128)S(1)}, /*index=5*/f32[100,768]{1,0:T(8,128)S(1)}) custom-call(s32[25]{0:T(128)S(1)} %stack.47.info.table, f32[100,512]{1,0:T(8,128)} %get-tuple-element.31.refs_0_, ...), custom_call_target="tpu_custom_call" | custom-call | flops 11059200 | bytes 3276800 | tf_op jit(solution)/shard_map/pairs/pallas_call | solution.py:167
  51.4 2.0 %collective-permute-start.9 = (f32[100,768]{1,0:T(8,128)S(1)}, f32[100,768]{1,0:T(8,128)S(1)}, u32[]{:S(2)}, u32[]{:S(2)}) collective-permute-start(f32[100,768]{1,0:T(8,128)S(1)} %get-tuple-element.41), channel_id=1, source_target_pairs={{48,0},{32,16},{80,32},{64,48},{112,64},{96,80},{16,96},{0,112},{4... | collective-permute-start | bytes 921608 | tf_op jit(solution)/shard_map/ppermute | solution.py:402
  54.1 1.3 collective-permute-start.11
  55.5 7.7 %collective-permute-done.7.left.refs_0_ = f32[100,768]{1,0:T(8,128)S(1)} collective-permute-done((f32[100,768]{1,0:T(8,128)S(1)}, f32[100,768]{1,0:T(8,128)S(1)}, u32[]{:S(2)}, u32[]{:S(2)}) %collective-permute-start.7) | collective-permute-done | bytes 307232 | tf_op jit(solution)/shard_map/ppermute | solution.py:402
  63.1 3.8 %collective-permute-start.12 = (f32[100,512]{1,0:T(8,128)S(1)}, f32[100,512]{1,0:T(8,128)S(1)}, u32[]{:S(2)}, u32[]{:S(2)}) collective-permute-start(f32[100,512]{1,0:T(8,128)S(1)} %join_tails.2), channel_id=1, source_target_pairs={{0,96},{32,0},{64,32},{96,64},{1,97},{33,1},{65,33},{97,65},{2,98}... | collective-permute-start | bytes 614408 | tf_op jit(solution)/shard_map/ppermute | solution.py:390
  67.1 2.9 %collective-permute-done.11.refs_5_ = f32[100,512]{1,0:T(8,128)S(1)} collective-permute-done((f32[100,512]{1,0:T(8,128)S(1)}, f32[100,512]{1,0:T(8,128)S(1)}, u32[]{:S(2)}, u32[]{:S(2)}) %collective-permute-start.11) | collective-permute-done | bytes 204832 | tf_op jit(solution)/shard_map/ppermute | solution.py:403
  70.0 3.1 %collective-permute-done.13.refs_7_ = f32[100,512]{1,0:T(8,128)S(1)} collective-permute-done((f32[100,512]{1,0:T(8,128)S(1)}, f32[100,512]{1,0:T(8,128)S(1)}, u32[]{:S(2)}, u32[]{:S(2)}) %collective-permute-start.13) | collective-permute-done | bytes 204832 | tf_op jit(solution)/shard_map/ppermute | solution.py:390
  73.1 20.1 %backward.1 = (bf16[8,1024,512]{2,1,0:T(8,128)(2,1)}, f32[64,8,1152]{2,1,0:T(8,128)S(1)}, f32[64,8,1152]{2,1,0:T(8,128)S(1)}) custom-call(s32[25]{0:T(128)S(1)} %stack.47.info.table, f32[100,768]{1,0:T(8,128)S(1)} %collective-permute-done.7.left.refs_0_, f32[100,768]{1,0:T(8,128)S(1)} %collective-permute-done.8.left.refs_1_, ...), custom_call_target="tpu_custom_call" | custom-call | flops 10267656192 | bytes 37748736 | tf_op jit(solution)/shard_map/backward/pallas_call | solution.py:274
  93.2 5.6 %collective-permute-start.14 = (f32[64,8,1152]{2,1,0:T(8,128)S(1)}, f32[64,8,1152]{2,1,0:T(8,128)S(1)}, u32[]{:S(2)}, u32[]{:S(2)}) collective-permute-start(f32[64,8,1152]{2,1,0:T(8,128)S(1)} %get-tuple-element.50), channel_id=1, source_target_pairs={{0,1},{1,0},{2,3},{3,2},{4,5},{5,4},{6,7},{7,6},{8,9},{9,8},{10,11... | collective-permute-start | bytes 7077896 | tf_op jit(solution)/shard_map/ppermute | solution.py:371
  98.8 4.2 %collective-permute-done.14 = f32[64,8,1152]{2,1,0:T(8,128)S(1)} collective-permute-done((f32[64,8,1152]{2,1,0:T(8,128)S(1)}, f32[64,8,1152]{2,1,0:T(8,128)S(1)}, u32[]{:S(2)}, u32[]{:S(2)}) %collective-permute-start.14) | collective-permute-done | bytes 2359328 | tf_op jit(solution)/shard_map/ppermute | solution.py:371
  103.0 1.7 %add.50 = f32[64,8,1152]{2,1,0:T(8,128)} add(f32[64,8,1152]{2,1,0:T(8,128)S(1)} %get-tuple-element.49, f32[64,8,1152]{2,1,0:T(8,128)S(1)} %collective-permute-done.14) | non-fusion elementwise | flops 589824 | bytes 7077888 | tf_op jit(solution)/shard_map/add | solution.py:372
  104.7 8.0 %all-to-all-start = ((f32[64,8,1152]{2,1,0:T(8,128)}), f32[64,8,1152]{2,1,0:T(8,128)S(1)}, u32[]{:S(2)}, u32[]{:S(2)}) async-start(f32[64,8,1152]{2,1,0:T(8,128)} %add.50), calls=%async_computation | async-start | bytes 4718592 | tf_op jit(solution)/shard_map/all_to_all | solution.py:372
  112.7 14.8 %feature_grad.1 = bf16[1,1024,4096]{2,1,0:T(8,128)(2,1)} custom-call(s32[25]{0:T(128)S(1)} %stack.47.info.table, bf16[1024,1024]{1,0:T(8,128)(2,1)} %w.1, bf16[8,1024,512]{2,1,0:T(8,128)(2,1)} %get-tuple-element.48.grad), custom_call_target="tpu_custom_call" | custom-call | flops 8589934592 | bytes 18874368 | tf_op jit(solution)/shard_map/feature_grad/pallas_call | solution.py:324
  127.4 17.6 %all-to-all-done.parts = f32[64,8,1152]{2,1,0:T(8,128)S(1)} async-done(((f32[64,8,1152]{2,1,0:T(8,128)}), f32[64,8,1152]{2,1,0:T(8,128)S(1)}, u32[]{:S(2)}, u32[]{:S(2)}) %all-to-all-start) | async-done | bytes 2359328 | tf_op jit(solution)/shard_map/all_to_all | solution.py:372
  (22 shorter events, 5.3 us)
Async XLA Ops:
  13.8 33.0 %copy-start = (bf16[100,4096]{1,0:T(8,128)(2,1)S(1)}, bf16[100,4096]{1,0:T(8,128)(2,1)}, u32[]{:S(2)}) copy-start(bf16[100,4096]{1,0:T(8,128)(2,1)} %refs_8_.1) | copy-start | bytes 2457604
  13.8 33.0 %copy-start.1 = (f32[4096]{0:T(1024)S(1)}, f32[4096]{0:T(1024)}, u32[]{:S(2)}) copy-start(f32[4096]{0:T(1024)} %param.9) | copy-start | bytes 49156
  21.7 9.5 %collective-permute-start.1 = (f32[100,512]{1,0:T(8,128)S(1)}, f32[100,512]{1,0:T(8,128)S(1)}, u32[]{:S(2)}, u32[]{:S(2)}) collective-permute-start(f32[100,512]{1,0:T(8,128)S(1)} %get-tuple-element.33), channel_id=1, source_target_pairs={{0,32},{16,48},{32,64},{48,80},{64,96},{80,112},{96,0},{112,16},{1... | collective-permute-start | bytes 614408 | tf_op jit(solution)/shard_map/ppermute | solution.py:398
  24.2 8.1 %collective-permute-start.2 = (f32[100,512]{1,0:T(8,128)S(1)}, f32[100,512]{1,0:T(8,128)S(1)}, u32[]{:S(2)}, u32[]{:S(2)}) collective-permute-start(f32[100,512]{1,0:T(8,128)S(1)} %get-tuple-element.34), channel_id=1, source_target_pairs={{0,96},{16,112},{32,0},{48,16},{64,32},{80,48},{96,64},{112,80},{1... | collective-permute-start | bytes 614408 | tf_op jit(solution)/shard_map/ppermute | solution.py:398
  26.3 8.9 %collective-permute-start = (f32[100,512]{1,0:T(8,128)S(1)}, f32[100,512]{1,0:T(8,128)S(1)}, u32[]{:S(2)}, u32[]{:S(2)}) collective-permute-start(f32[100,512]{1,0:T(8,128)S(1)} %get-tuple-element.32), channel_id=1, source_target_pairs={{0,16},{16,0},{32,48},{48,32},{64,80},{80,64},{96,112},{112,96},{1... | collective-permute-start | bytes 614408 | tf_op jit(solution)/shard_map/ppermute | solution.py:395
  27.6 10.0 %collective-permute-start.3 = (f32[100,512]{1,0:T(8,128)S(1)}, f32[100,512]{1,0:T(8,128)S(1)}, u32[]{:S(2)}, u32[]{:S(2)}) collective-permute-start(f32[100,512]{1,0:T(8,128)S(1)} %get-tuple-element.35), channel_id=1, source_target_pairs={{0,48},{16,32},{32,80},{48,64},{64,112},{80,96},{96,16},{112,0},{1... | collective-permute-start | bytes 614408 | tf_op jit(solution)/shard_map/ppermute | solution.py:395
  27.6 12.9 %collective-permute-start.4 = (f32[100,512]{1,0:T(8,128)S(1)}, f32[100,512]{1,0:T(8,128)S(1)}, u32[]{:S(2)}, u32[]{:S(2)}) collective-permute-start(f32[100,512]{1,0:T(8,128)S(1)} %get-tuple-element.36), channel_id=1, source_target_pairs={{0,112},{16,96},{32,16},{48,0},{64,48},{80,32},{96,80},{112,64},{1... | collective-permute-start | bytes 614408 | tf_op jit(solution)/shard_map/ppermute | solution.py:395
  31.2 12.2 %collective-permute-start.5 = (f32[100,512]{1,0:T(8,128)S(1)}, f32[100,512]{1,0:T(8,128)S(1)}, u32[]{:S(2)}, u32[]{:S(2)}) collective-permute-start(f32[100,512]{1,0:T(8,128)S(1)} %get-tuple-element.37), channel_id=1, source_target_pairs={{0,64},{16,80},{32,96},{48,112},{64,0},{80,16},{96,32},{112,48},{1... | collective-permute-start | bytes 614408 | tf_op jit(solution)/shard_map/ppermute | solution.py:395
  32.3 14.5 %collective-permute-start.6 = (f32[100,512]{1,0:T(8,128)S(1)}, f32[100,512]{1,0:T(8,128)S(1)}, u32[]{:S(2)}, u32[]{:S(2)}) collective-permute-start(f32[100,512]{1,0:T(8,128)S(1)} %get-tuple-element.38), channel_id=1, source_target_pairs={{0,80},{16,64},{32,112},{48,96},{64,16},{80,0},{96,48},{112,32},{1... | collective-permute-start | bytes 614408 | tf_op jit(solution)/shard_map/ppermute | solution.py:395
  50.2 12.9 %collective-permute-start.7 = (f32[100,768]{1,0:T(8,128)S(1)}, f32[100,768]{1,0:T(8,128)S(1)}, u32[]{:S(2)}, u32[]{:S(2)}) collective-permute-start(f32[100,768]{1,0:T(8,128)S(1)} %get-tuple-element.39), channel_id=1, source_target_pairs={{32,0},{48,16},{64,32},{80,48},{96,64},{112,80},{0,96},{16,112},{3... | collective-permute-start | bytes 921608 | tf_op jit(solution)/shard_map/ppermute | solution.py:402
  51.4 11.7 %collective-permute-start.9 = (f32[100,768]{1,0:T(8,128)S(1)}, f32[100,768]{1,0:T(8,128)S(1)}, u32[]{:S(2)}, u32[]{:S(2)}) collective-permute-start(f32[100,768]{1,0:T(8,128)S(1)} %get-tuple-element.41), channel_id=1, source_target_pairs={{48,0},{32,16},{80,32},{64,48},{112,64},{96,80},{16,96},{0,112},{4... | collective-permute-start | bytes 921608 | tf_op jit(solution)/shard_map/ppermute | solution.py:402
  53.4 13.6 %collective-permute-start.8 = (f32[100,768]{1,0:T(8,128)S(1)}, f32[100,768]{1,0:T(8,128)S(1)}, u32[]{:S(2)}, u32[]{:S(2)}) collective-permute-start(f32[100,768]{1,0:T(8,128)S(1)} %get-tuple-element.40), channel_id=1, source_target_pairs={{96,0},{112,16},{0,32},{16,48},{32,64},{48,80},{64,96},{80,112},{9... | collective-permute-start | bytes 921608 | tf_op jit(solution)/shard_map/ppermute | solution.py:402
  53.9 13.1 %collective-permute-start.10 = (f32[100,768]{1,0:T(8,128)S(1)}, f32[100,768]{1,0:T(8,128)S(1)}, u32[]{:S(2)}, u32[]{:S(2)}) collective-permute-start(f32[100,768]{1,0:T(8,128)S(1)} %get-tuple-element.42), channel_id=1, source_target_pairs={{112,0},{96,16},{16,32},{0,48},{48,64},{32,80},{80,96},{64,112},{1... | collective-permute-start | bytes 921608 | tf_op jit(solution)/shard_map/ppermute | solution.py:402
  54.1 15.9 %collective-permute-start.11 = (f32[100,512]{1,0:T(8,128)S(1)}, f32[100,512]{1,0:T(8,128)S(1)}, u32[]{:S(2)}, u32[]{:S(2)}) collective-permute-start(f32[100,512]{1,0:T(8,128)S(1)} %get-tuple-element.44), channel_id=1, source_target_pairs={{16,0},{0,16},{48,32},{32,48},{80,64},{64,80},{112,96},{96,112},{1... | collective-permute-start | bytes 614408 | tf_op jit(solution)/shard_map/ppermute | solution.py:403
  63.1 6.9 %collective-permute-start.12 = (f32[100,512]{1,0:T(8,128)S(1)}, f32[100,512]{1,0:T(8,128)S(1)}, u32[]{:S(2)}, u32[]{:S(2)}) collective-permute-start(f32[100,512]{1,0:T(8,128)S(1)} %join_tails.2), channel_id=1, source_target_pairs={{0,96},{32,0},{64,32},{96,64},{1,97},{33,1},{65,33},{97,65},{2,98}... | collective-permute-start | bytes 614408 | tf_op jit(solution)/shard_map/ppermute | solution.py:390
  67.0 6.1 %collective-permute-start.13 = (f32[100,512]{1,0:T(8,128)S(1)}, f32[100,512]{1,0:T(8,128)S(1)}, u32[]{:S(2)}, u32[]{:S(2)}) collective-permute-start(f32[100,512]{1,0:T(8,128)S(1)} %join_tails.3), channel_id=1, source_target_pairs={{0,32},{32,64},{64,96},{96,0},{1,33},{33,65},{65,97},{97,1},{2,34}... | collective-permute-start | bytes 614408 | tf_op jit(solution)/shard_map/ppermute | solution.py:390
  93.2 9.8 %collective-permute-start.14 = (f32[64,8,1152]{2,1,0:T(8,128)S(1)}, f32[64,8,1152]{2,1,0:T(8,128)S(1)}, u32[]{:S(2)}, u32[]{:S(2)}) collective-permute-start(f32[64,8,1152]{2,1,0:T(8,128)S(1)} %get-tuple-element.50), channel_id=1, source_target_pairs={{0,1},{1,0},{2,3},{3,2},{4,5},{5,4},{6,7},{7,6},{8,9},{9,8},{10,11... | collective-permute-start | bytes 7077896 | tf_op jit(solution)/shard_map/ppermute | solution.py:371
  104.7 40.3 %all-to-all-start = ((f32[64,8,1152]{2,1,0:T(8,128)}), f32[64,8,1152]{2,1,0:T(8,128)S(1)}, u32[]{:S(2)}, u32[]{:S(2)}) async-start(f32[64,8,1152]{2,1,0:T(8,128)} %add.50), calls=%async_computation | async-start | bytes 4718592 | tf_op jit(solution)/shard_map/all_to_all | solution.py:372
where the time goes:
time: 146 us
  Pallas kernels  60 us (41%)
  waiting for transfers between devices  47.1 us (32%)
  starting transfers between devices  36.2 us (25%)
  other arithmetic  1.72 us (1%)
    pallas_call x2, Pallas kernels, forward(): pl.pallas_call(functools.partial(forward_kernel, first), grid_spec=pltpu....  20.9 us
    pallas_call x1, Pallas kernels, backward(): pl.pallas_call(backward_kernel, grid_spec=pltpu.PrefetchScalarGridSpec(nu...  20.1 us
    all_to_all x1, waiting for transfers between devices, spread(): return lax.all_to_all(keep + swapped, CHIP, 0, 0, tiled=True)  17.6 us
    pallas_call x1, Pallas kernels, feature_grad(): pl.pallas_call(feature_kernel, grid_spec=pltpu.PrefetchScalarGridSpec(num...  14.8 us
    ppermute x5, waiting for transfers between devices, body(): got[s] = lax.ppermute(p, MEMBER, route(s, False))  11.6 us
    ppermute x5, starting transfers between devices, body(): got[s] = lax.ppermute(p, MEMBER, route(s, False))  8.85 us
    all_to_all x1, starting transfers between devices, spread(): return lax.all_to_all(keep + swapped, CHIP, 0, 0, tiled=True)  7.97 us
    ppermute x4, waiting for transfers between devices, body(): lax.ppermute(block, MEMBER, route(s, True))  7.67 us
  transfers between devices with their start and end apart: 16, of which 10 were waited for; matrix products, arithmetic and copies ran while one was open for 0% of the time, Pallas kernels for 10%

commit v1 on v0

--- a/solution.py
+++ b/solution.py
@@ -19,9 +19,8 @@
 SIDE = ((0, 0), (0, 1))
 FAR = ((2, 0), (2, 1))
 SLOTS = NEAR + SIDE + FAR
-FIRST = ((2, 1), (2, 0), (1, 1), (3, 1), (0, 1))
-SECOND = ((1, 0), (3, 0), (0, 0))
-ORDER = FIRST + SECOND
+GROUPS = (((2, 1), (2, 0)), ((1, 1), (3, 1), (0, 1)), ((1, 0), (3, 0), (0, 0)))
+ORDER = GROUPS[0] + GROUPS[1] + GROUPS[2]
 
 TILE = 512
 SPAN = 1024
@@ -57,7 +56,7 @@
     return lax.dot_general(a, b, (((ca,), (cb,)), ((), ())), preferred_element_type=F32)
 
 
-def forward_kernel(first, info, *refs):
+def forward_kernel(first, base, info, *refs):
     if first:
         x, w, owt, hidden, slope, *preds, wt, ow = refs
     else:
@@ -72,7 +71,7 @@
                 wt[:, i : i + ROWS] = (w[i : i + ROWS, :] * 0.5).T
             ow[...] = (owt[...] * 0.5).T
 
-    slot = info[17 + (0 if first else len(FIRST)) + step]
+    slot = info[17 + base + step]
     h = mm(wt[...], x[...], 1, 0)
     u = jnp.tanh(h) + 1.0
     act = h * u
@@ -87,11 +86,11 @@
             out[...] = pred
 
 
-def forward(info, x, w, owt, carried=None):
+def forward(group, info, x, w, owt, carried=None):
     first = carried is None
     depth, _ = x.shape
     channels = owt.shape[0]
-    n, base = (len(FIRST), 0) if first else (len(SECOND), len(FIRST))
+    n, base = len(GROUPS[group]), ORDER.index(GROUPS[group][0])
     at_tile = pl.BlockSpec((depth, TILE), lambda g, t: (0, t[9 + base + g]))
     whole = lambda *s: pl.BlockSpec(s, lambda g, t: (0,) * len(s))
     fixed = pl.BlockSpec(memory_space=pltpu.VMEM)
@@ -106,13 +105,14 @@
         out_shape += [pltpu.VMEM((depth, depth), BF16), pltpu.HBM((depth, channels), BF16)]
         out_specs += [fixed, whole(depth, channels)]
     else:
-        out_shape[-1] = pltpu.HBM((channels, TILE), F32)
-        out_specs[-1] = whole(channels, TILE)
+        if (0, 0) in GROUPS[group]:
+            out_shape[-1] = pltpu.HBM((channels, TILE), F32)
+            out_specs[-1] = whole(channels, TILE)
         args += map(in_vmem, carried)
         in_specs += [fixed, fixed]
         alias = {4: 0, 5: 1}
     return pl.pallas_call(
-        functools.partial(forward_kernel, first),
+        functools.partial(forward_kernel, first, base),
         grid_spec=pltpu.PrefetchScalarGridSpec(
             num_scalar_prefetch=1, grid=(n,), in_specs=in_specs, out_specs=out_specs
         ),
@@ -389,12 +389,13 @@
     def relay(blocks, step):
         return lax.ppermute(join_tails(*blocks), "z", [(i, (i + step) % 4) for i in range(4)])
 
-    hidden, slope, *sent, wt, ow = forward(info, x, up_weight, owt)
+    hidden, slope, *sent, wt, ow = forward(0, info, x, up_weight, owt)
     got = {}
-    for s, p in zip(FIRST, sent):
-        got[s] = lax.ppermute(p, MEMBER, route(s, False))
-    hidden, slope, *sent = forward(info, x, wt, owt, (hidden, slope))
-    for s, p in zip(SECOND, sent):
+    for group in (1, 2):
+        for s, p in zip(GROUPS[group - 1], sent):
+            got[s] = lax.ppermute(p, MEMBER, route(s, False))
+        hidden, slope, *sent = forward(group, info, x, wt, owt, (hidden, slope))
+    for s, p in zip(GROUPS[2], sent):
         got[s] = p if s == (0, 0) else lax.ppermute(p, MEMBER, route(s, False))
     order = SIDE + NEAR + FAR
     own, side, *sent = pairs(info, [got[s] for s in order], target, area[None, :])

time: 146 us -> 154 us (1.055)
  local copies, waits for them, and re-layouts: 0.11 us -> 6.89 us
  starting transfers between devices: 36.2 us -> 34.4 us
  Pallas kernels: 60 us -> 61.8 us
    unnamed x4 -> x8, local copies, waits for them, and re-layouts: 0.01 us -> 6.79 us
    ppermute x4, waiting for transfers between devices: 7.67 us -> 10.5 us  [body(): lax.ppermute(block, MEMBER, route(s, True))]
    ppermute x5, waiting for transfers between devices: 11.6 us -> 9.18 us  [body(): got[s] = lax.ppermute(p, MEMBER, route(s, False))]
    ppermute x1, starting transfers between devices: 5.63 us -> 3.27 us  [spread(): swapped = lax.ppermute(away, 'core', [(0, 1), (1, 0)])]
    ppermute x1, waiting for transfers between devices: 2.93 us -> 0.65 us  [body(): side = lax.ppermute(side, MEMBER, route((0, 1), True))]
    ppermute x2, waiting for transfers between devices: 3.08 us -> 5.24 us  [relay(): lax.ppermute(join_tails(*blocks), 'z', [(i, (i + step) % 4) for i in rang...]
    ppermute x4, starting transfers between devices: 3.9 us -> 5.68 us  [body(): lax.ppermute(block, MEMBER, route(s, True))]
    pallas_call x2 -> x3, Pallas kernels: 20.9 us -> 22.6 us  [forward(): pl.pallas_call(functools.partial(forward_kernel, first, base), grid_spec=...]
  transfers between devices with their start and end apart: 16 -> 16, of which waited for: 10 -> 10; matrix products, arithmetic and copies ran while one was open for 0% -> 0% of each run, Pallas kernels for 10% -> 19%
where the time goes in v1:
time: 154 us
  Pallas kernels  61.8 us (40%)
  waiting for transfers between devices  47.9 us (31%)
  starting transfers between devices  34.4 us (22%)
  local copies, waits for them, and re-layouts  6.89 us (4%)
  other arithmetic  1.83 us (1%)
    pallas_call x3, Pallas kernels, forward(): pl.pallas_call(functools.partial(forward_kernel, first, base), grid_spec=...  22.6 us
    pallas_call x1, Pallas kernels, backward(): pl.pallas_call(backward_kernel, grid_spec=pltpu.PrefetchScalarGridSpec(nu...  20.1 us
    all_to_all x1, waiting for transfers between devices, spread(): return lax.all_to_all(keep + swapped, CHIP, 0, 0, tiled=True)  17.6 us
    pallas_call x1, Pallas kernels, feature_grad(): pl.pallas_call(feature_kernel, grid_spec=pltpu.PrefetchScalarGridSpec(num...  14.8 us
    ppermute x4, waiting for transfers between devices, body(): lax.ppermute(block, MEMBER, route(s, True))  10.5 us
    ppermute x5, waiting for transfers between devices, body(): got[s] = lax.ppermute(p, MEMBER, route(s, False))  9.18 us
    ppermute x5, starting transfers between devices, body(): got[s] = lax.ppermute(p, MEMBER, route(s, False))  9.18 us
    all_to_all x1, starting transfers between devices, spread(): return lax.all_to_all(keep + swapped, CHIP, 0, 0, tiled=True)  9.11 us
  transfers between devices with their start and end apart: 16, of which 10 were waited for; matrix products, arithmetic and copies ran while one was open for 0% of the time, Pallas kernels for 19%

profile of v1, /device:TPU:1, one launch (start us, length us, event | category | flops | bytes accessed | tf_op | source)
XLA Modules:
  0.0 153.5 jit_solution(4280728871185015432)
XLA Ops:
  0.8 7.5 %forward.3 = (bf16[8,1024,512]{2,1,0:T(8,128)(2,1)S(1)}, bf16[8,1024,512]{2,1,0:T(8,128)(2,1)S(1)}, f32[100,512]{1,0:T(8,128)S(1)}, f32[100,512]{1,0:T(8,128)S(1...) custom-call(s32[25]{0:T(128)S(1)} %stack.47.info.table, bf16[1024,4096]{1,0:T(8,128)(2,1)} %bitcast.13, ...), custom_call_target="tpu_custom_call" | custom-call | flops 2357198848 | bytes 8388608 | tf_op jit(solution)/shard_map/forward/pallas_call | solution.py:114
  8.3 4.4 %collective-permute-start.5 = (f32[100,512]{1,0:T(8,128)S(1)}, f32[100,512]{1,0:T(8,128)S(1)}, u32[]{:S(2)}, u32[]{:S(2)}) collective-permute-start(f32[100,512]{1,0:T(8,128)S(1)} %get-tuple-element.41), channel_id=1, source_target_pairs={{0,64},{16,80},{32,96},{48,112},{64,0},{80,16},{96,32},{112,48},{1... | collective-permute-start | bytes 614408 | tf_op jit(solution)/shard_map/ppermute | solution.py:396
  13.7 7.2 %forward.4 = (bf16[8,1024,512]{2,1,0:T(8,128)(2,1)S(1)}, bf16[8,1024,512]{2,1,0:T(8,128)(2,1)S(1)}, f32[100,512]{1,0:T(8,128)S(1)}, f32[100,512]{1,0:T(8,128)S(1)}, f32[100,512]{1,0:T(8,128)S(1)}) custom-call(s32[25]{0:T(128)S(1)} %stack.47.info.table, bf16[1024,4096]{1,0:T(8,128)(2,1)} %bitcast.14, ...), custom_call_target="tpu_custom_call", output_to_operand_aliasing={{0}: (4, {}), {1}: (5, {})} | custom-call | flops 3535798272 | bytes 11534336 | tf_op jit(solution)/shard_map/forward/pallas_call | solution.py:114
  21.0 7.9 %forward.5 = (bf16[8,1024,512]{2,1,0:T(8,128)(2,1)S(1)}, bf16[8,1024,512]{2,1,0:T(8,128)(2,1)S(1)}, f32[100,512]{1,0:T(8,128)S(1)}, f32[100,512]{1,0:T(8,128)S(1)}, f32[100,512]{1,0:T(8,128)}) custom-call(s32[25]{0:T(128)S(1)} %stack.47.info.table, bf16[1024,4096]{1,0:T(8,128)(2,1)} %bitcast.15, ...), custom_call_target="tpu_custom_call", output_to_operand_aliasing={{0}: (4, {}), {1}: (5, {})} | custom-call | flops 3535798272 | bytes 11534336 | tf_op jit(solution)/shard_map/forward/pallas_call | solution.py:114
  28.9 3.4 %copy-done = bf16[8,1024,512]{2,1,0:T(8,128)(2,1)} copy-done((bf16[8,1024,512]{2,1,0:T(8,128)(2,1)}, bf16[8,1024,512]{2,1,0:T(8,128)(2,1)S(1)}, u32[]{:S(2)}) %copy-start) | copy-done | bytes 8388632
  33.3 2.1 %collective-permute-start.2 = (f32[100,512]{1,0:T(8,128)S(1)}, f32[100,512]{1,0:T(8,128)S(1)}, u32[]{:S(2)}, u32[]{:S(2)}) collective-permute-start(f32[100,512]{1,0:T(8,128)S(1)} %get-tuple-element.38), channel_id=1, source_target_pairs={{0,96},{16,112},{32,0},{48,16},{64,32},{80,48},{96,64},{112,80},{1... | collective-permute-start | bytes 614408 | tf_op jit(solution)/shard_map/ppermute | solution.py:399
  36.1 3.0 %collective-permute-start.4 = (f32[100,512]{1,0:T(8,128)S(1)}, f32[100,512]{1,0:T(8,128)S(1)}, u32[]{:S(2)}, u32[]{:S(2)}) collective-permute-start(f32[100,512]{1,0:T(8,128)S(1)} %get-tuple-element.40), channel_id=1, source_target_pairs={{0,112},{16,96},{32,16},{48,0},{64,48},{80,32},{96,80},{112,64},{1... | collective-permute-start | bytes 614408 | tf_op jit(solution)/shard_map/ppermute | solution.py:396
  40.7 5.5 %collective-permute-done.3.refs_4_ = f32[100,512]{1,0:T(8,128)S(1)} collective-permute-done((f32[100,512]{1,0:T(8,128)S(1)}, f32[100,512]{1,0:T(8,128)S(1)}, u32[]{:S(2)}, u32[]{:S(2)}) %collective-permute-start.3) | collective-permute-done | bytes 204832 | tf_op jit(solution)/shard_map/ppermute | solution.py:396
  46.1 2.8 %collective-permute-done.4.refs_5_ = f32[100,512]{1,0:T(8,128)S(1)} collective-permute-done((f32[100,512]{1,0:T(8,128)S(1)}, f32[100,512]{1,0:T(8,128)S(1)}, u32[]{:S(2)}, u32[]{:S(2)}) %collective-permute-start.4) | collective-permute-done | bytes 204832 | tf_op jit(solution)/shard_map/ppermute | solution.py:396
  49.0 3.4 %pairs.1 = (f32[100,512]{1,0:T(8,128)}, f32[100,512]{1,0:T(8,128)S(1)}, f32[100,768]{1,0:T(8,128)S(1)}, f32[100,768]{1,0:T(8,128)S(1)}, f32[100,768]{1,0:T(8,128)S(1)}, /*index=5*/f32[100,768]{1,0:T(8,128)S(1)}) custom-call(s32[25]{0:T(128)S(1)} %stack.47.info.table, f32[100,512]{1,0:T(8,128)} %get-tuple-element.35.refs_0_, ...), custom_call_target="tpu_custom_call" | custom-call | flops 11059200 | bytes 3276800 | tf_op jit(solution)/shard_map/pairs/pallas_call | solution.py:167
  52.4 3.3 %collective-permute-start.7 = (f32[100,768]{1,0:T(8,128)S(1)}, f32[100,768]{1,0:T(8,128)S(1)}, u32[]{:S(2)}, u32[]{:S(2)}) collective-permute-start(f32[100,768]{1,0:T(8,128)S(1)} %get-tuple-element.43), channel_id=1, source_target_pairs={{32,0},{48,16},{64,32},{80,48},{96,64},{112,80},{0,96},{16,112},{3... | collective-permute-start | bytes 921608 | tf_op jit(solution)/shard_map/ppermute | solution.py:403
  55.7 1.3 collective-permute-start.8
  58.4 10.5 %collective-permute-done.7.left.refs_0_ = f32[100,768]{1,0:T(8,128)S(1)} collective-permute-done((f32[100,768]{1,0:T(8,128)S(1)}, f32[100,768]{1,0:T(8,128)S(1)}, u32[]{:S(2)}, u32[]{:S(2)}) %collective-permute-start.7) | collective-permute-done | bytes 307232 | tf_op jit(solution)/shard_map/ppermute | solution.py:403
  68.9 3.5 %collective-permute-start.12 = (f32[100,512]{1,0:T(8,128)S(1)}, f32[100,512]{1,0:T(8,128)S(1)}, u32[]{:S(2)}, u32[]{:S(2)}) collective-permute-start(f32[100,512]{1,0:T(8,128)S(1)} %join_tails.2), channel_id=1, source_target_pairs={{0,96},{32,0},{64,32},{96,64},{1,97},{33,1},{65,33},{97,65},{2,98}... | collective-permute-start | bytes 614408 | tf_op jit(solution)/shard_map/ppermute | solution.py:390
  73.3 2.2 %collective-permute-done.12.refs_6_ = f32[100,512]{1,0:T(8,128)S(1)} collective-permute-done((f32[100,512]{1,0:T(8,128)S(1)}, f32[100,512]{1,0:T(8,128)S(1)}, u32[]{:S(2)}, u32[]{:S(2)}) %collective-permute-start.12) | collective-permute-done | bytes 204832 | tf_op jit(solution)/shard_map/ppermute | solution.py:390
  75.5 3.0 %collective-permute-done.13.refs_7_ = f32[100,512]{1,0:T(8,128)S(1)} collective-permute-done((f32[100,512]{1,0:T(8,128)S(1)}, f32[100,512]{1,0:T(8,128)S(1)}, u32[]{:S(2)}, u32[]{:S(2)}) %collective-permute-start.13) | collective-permute-done | bytes 204832 | tf_op jit(solution)/shard_map/ppermute | solution.py:390
  78.5 3.4 %copy-done.1 = bf16[8,1024,512]{2,1,0:T(8,128)(2,1)S(1)} copy-done((bf16[8,1024,512]{2,1,0:T(8,128)(2,1)S(1)}, bf16[8,1024,512]{2,1,0:T(8,128)(2,1)}, u32[]{:S(2)}) %copy-start.1) | copy-done | bytes 8388632
  81.9 20.1 %backward.1 = (bf16[8,1024,512]{2,1,0:T(8,128)(2,1)}, f32[64,8,1152]{2,1,0:T(8,128)S(1)}, f32[64,8,1152]{2,1,0:T(8,128)S(1)}) custom-call(s32[25]{0:T(128)S(1)} %stack.47.info.table, f32[100,768]{1,0:T(8,128)S(1)} %collective-permute-done.7.left.refs_0_, f32[100,768]{1,0:T(8,128)S(1)} %collective-permute-done.8.left.refs_1_, ...), custom_call_target="tpu_custom_call" | custom-call | flops 10267656192 | bytes 37748736 | tf_op jit(solution)/shard_map/backward/pallas_call | solution.py:274
  102.1 3.3 %collective-permute-start.14 = (f32[64,8,1152]{2,1,0:T(8,128)S(1)}, f32[64,8,1152]{2,1,0:T(8,128)S(1)}, u32[]{:S(2)}, u32[]{:S(2)}) collective-permute-start(f32[64,8,1152]{2,1,0:T(8,128)S(1)} %get-tuple-element.54), channel_id=1, source_target_pairs={{0,1},{1,0},{2,3},{3,2},{4,5},{5,4},{6,7},{7,6},{8,9},{9,8},{10,11... | collective-permute-start | bytes 7077896 | tf_op jit(solution)/shard_map/ppermute | solution.py:371
  105.3 4.2 %collective-permute-done.14 = f32[64,8,1152]{2,1,0:T(8,128)S(1)} collective-permute-done((f32[64,8,1152]{2,1,0:T(8,128)S(1)}, f32[64,8,1152]{2,1,0:T(8,128)S(1)}, u32[]{:S(2)}, u32[]{:S(2)}) %collective-permute-start.14) | collective-permute-done | bytes 2359328 | tf_op jit(solution)/shard_map/ppermute | solution.py:371
  109.5 1.8 %add.50 = f32[64,8,1152]{2,1,0:T(8,128)} add(f32[64,8,1152]{2,1,0:T(8,128)S(1)} %get-tuple-element.53, f32[64,8,1152]{2,1,0:T(8,128)S(1)} %collective-permute-done.14) | non-fusion elementwise | flops 589824 | bytes 7077888 | tf_op jit(solution)/shard_map/add | solution.py:372
  111.3 9.1 %all-to-all-start = ((f32[64,8,1152]{2,1,0:T(8,128)}), f32[64,8,1152]{2,1,0:T(8,128)S(1)}, u32[]{:S(2)}, u32[]{:S(2)}) async-start(f32[64,8,1152]{2,1,0:T(8,128)} %add.50), calls=%async_computation | async-start | bytes 4718592 | tf_op jit(solution)/shard_map/all_to_all | solution.py:372
  120.4 14.8 %feature_grad.1 = bf16[1,1024,4096]{2,1,0:T(8,128)(2,1)} custom-call(s32[25]{0:T(128)S(1)} %stack.47.info.table, bf16[1024,1024]{1,0:T(8,128)(2,1)} %w.1, bf16[8,1024,512]{2,1,0:T(8,128)(2,1)} %get-tuple-element.52.grad), custom_call_target="tpu_custom_call" | custom-call | flops 8589934592 | bytes 18874368 | tf_op jit(solution)/shard_map/feature_grad/pallas_call | solution.py:324
  135.2 17.6 %all-to-all-done.parts = f32[64,8,1152]{2,1,0:T(8,128)S(1)} async-done(((f32[64,8,1152]{2,1,0:T(8,128)}), f32[64,8,1152]{2,1,0:T(8,128)S(1)}, u32[]{:S(2)}, u32[]{:S(2)}) %all-to-all-start) | async-done | bytes 2359328 | tf_op jit(solution)/shard_map/all_to_all | solution.py:372
  (27 shorter events, 7.4 us)
Async XLA Ops:
  8.3 27.3 %collective-permute-start.5 = (f32[100,512]{1,0:T(8,128)S(1)}, f32[100,512]{1,0:T(8,128)S(1)}, u32[]{:S(2)}, u32[]{:S(2)}) collective-permute-start(f32[100,512]{1,0:T(8,128)S(1)} %get-tuple-element.41), channel_id=1, source_target_pairs={{0,64},{16,80},{32,96},{48,112},{64,0},{80,16},{96,32},{112,48},{1... | collective-permute-start | bytes 614408 | tf_op jit(solution)/shard_map/ppermute | solution.py:396
  12.7 23.4 %collective-permute-start.6 = (f32[100,512]{1,0:T(8,128)S(1)}, f32[100,512]{1,0:T(8,128)S(1)}, u32[]{:S(2)}, u32[]{:S(2)}) collective-permute-start(f32[100,512]{1,0:T(8,128)S(1)} %get-tuple-element.42), channel_id=1, source_target_pairs={{0,80},{16,64},{32,112},{48,96},{64,16},{80,0},{96,48},{112,32},{1... | collective-permute-start | bytes 614408 | tf_op jit(solution)/shard_map/ppermute | solution.py:396
  20.9 28.0 %copy-start.2 = (bf16[100,4096]{1,0:T(8,128)(2,1)S(1)}, bf16[100,4096]{1,0:T(8,128)(2,1)}, u32[]{:S(2)}) copy-start(bf16[100,4096]{1,0:T(8,128)(2,1)} %refs_8_.1) | copy-start | bytes 2457604
  20.9 28.0 %copy-start.3 = (f32[4096]{0:T(1024)S(1)}, f32[4096]{0:T(1024)}, u32[]{:S(2)}) copy-start(f32[4096]{0:T(1024)} %param.9) | copy-start | bytes 49156
  28.9 3.4 %copy-start = (bf16[8,1024,512]{2,1,0:T(8,128)(2,1)}, bf16[8,1024,512]{2,1,0:T(8,128)(2,1)S(1)}, u32[]{:S(2)}) copy-start(bf16[8,1024,512]{2,1,0:T(8,128)(2,1)S(1)} %get-tuple-element.50.refs_10_) | copy-start | bytes 25165828
  32.2 7.5 %collective-permute-start.1 = (f32[100,512]{1,0:T(8,128)S(1)}, f32[100,512]{1,0:T(8,128)S(1)}, u32[]{:S(2)}, u32[]{:S(2)}) collective-permute-start(f32[100,512]{1,0:T(8,128)S(1)} %get-tuple-element.37), channel_id=1, source_target_pairs={{0,32},{16,48},{32,64},{48,80},{64,96},{80,112},{96,0},{112,16},{1... | collective-permute-start | bytes 614408 | tf_op jit(solution)/shard_map/ppermute | solution.py:399
  33.3 6.5 %collective-permute-start.2 = (f32[100,512]{1,0:T(8,128)S(1)}, f32[100,512]{1,0:T(8,128)S(1)}, u32[]{:S(2)}, u32[]{:S(2)}) collective-permute-start(f32[100,512]{1,0:T(8,128)S(1)} %get-tuple-element.38), channel_id=1, source_target_pairs={{0,96},{16,112},{32,0},{48,16},{64,32},{80,48},{96,64},{112,80},{1... | collective-permute-start | bytes 614408 | tf_op jit(solution)/shard_map/ppermute | solution.py:399
  35.4 5.3 %collective-permute-start = (f32[100,512]{1,0:T(8,128)S(1)}, f32[100,512]{1,0:T(8,128)S(1)}, u32[]{:S(2)}, u32[]{:S(2)}) collective-permute-start(f32[100,512]{1,0:T(8,128)S(1)} %get-tuple-element.36), channel_id=1, source_target_pairs={{0,16},{16,0},{32,48},{48,32},{64,80},{80,64},{96,112},{112,96},{1... | collective-permute-start | bytes 614408 | tf_op jit(solution)/shard_map/ppermute | solution.py:396
  35.5 10.6 %collective-permute-start.3 = (f32[100,512]{1,0:T(8,128)S(1)}, f32[100,512]{1,0:T(8,128)S(1)}, u32[]{:S(2)}, u32[]{:S(2)}) collective-permute-start(f32[100,512]{1,0:T(8,128)S(1)} %get-tuple-element.39), channel_id=1, source_target_pairs={{0,48},{16,32},{32,80},{48,64},{64,112},{80,96},{96,16},{112,0},{1... | collective-permute-start | bytes 614408 | tf_op jit(solution)/shard_map/ppermute | solution.py:396
  36.1 12.8 %collective-permute-start.4 = (f32[100,512]{1,0:T(8,128)S(1)}, f32[100,512]{1,0:T(8,128)S(1)}, u32[]{:S(2)}, u32[]{:S(2)}) collective-permute-start(f32[100,512]{1,0:T(8,128)S(1)} %get-tuple-element.40), channel_id=1, source_target_pairs={{0,112},{16,96},{32,16},{48,0},{64,48},{80,32},{96,80},{112,64},{1... | collective-permute-start | bytes 614408 | tf_op jit(solution)/shard_map/ppermute | solution.py:396
  52.4 16.4 %collective-permute-start.7 = (f32[100,768]{1,0:T(8,128)S(1)}, f32[100,768]{1,0:T(8,128)S(1)}, u32[]{:S(2)}, u32[]{:S(2)}) collective-permute-start(f32[100,768]{1,0:T(8,128)S(1)} %get-tuple-element.43), channel_id=1, source_target_pairs={{32,0},{48,16},{64,32},{80,48},{96,64},{112,80},{0,96},{16,112},{3... | collective-permute-start | bytes 921608 | tf_op jit(solution)/shard_map/ppermute | solution.py:403
  55.7 13.1 %collective-permute-start.9 = (f32[100,768]{1,0:T(8,128)S(1)}, f32[100,768]{1,0:T(8,128)S(1)}, u32[]{:S(2)}, u32[]{:S(2)}) collective-permute-start(f32[100,768]{1,0:T(8,128)S(1)} %get-tuple-element.45), channel_id=1, source_target_pairs={{48,0},{32,16},{80,32},{64,48},{112,64},{96,80},{16,96},{0,112},{4... | collective-permute-start | bytes 921608 | tf_op jit(solution)/shard_map/ppermute | solution.py:403
  55.7 16.6 %collective-permute-start.8 = (f32[100,768]{1,0:T(8,128)S(1)}, f32[100,768]{1,0:T(8,128)S(1)}, u32[]{:S(2)}, u32[]{:S(2)}) collective-permute-start(f32[100,768]{1,0:T(8,128)S(1)} %get-tuple-element.44), channel_id=1, source_target_pairs={{96,0},{112,16},{0,32},{16,48},{32,64},{48,80},{64,96},{80,112},{9... | collective-permute-start | bytes 921608 | tf_op jit(solution)/shard_map/ppermute | solution.py:403
  57.1 15.3 %collective-permute-start.10 = (f32[100,768]{1,0:T(8,128)S(1)}, f32[100,768]{1,0:T(8,128)S(1)}, u32[]{:S(2)}, u32[]{:S(2)}) collective-permute-start(f32[100,768]{1,0:T(8,128)S(1)} %get-tuple-element.46), channel_id=1, source_target_pairs={{112,0},{96,16},{16,32},{0,48},{48,64},{32,80},{80,96},{64,112},{1... | collective-permute-start | bytes 921608 | tf_op jit(solution)/shard_map/ppermute | solution.py:403
  58.1 15.2 %collective-permute-start.11 = (f32[100,512]{1,0:T(8,128)S(1)}, f32[100,512]{1,0:T(8,128)S(1)}, u32[]{:S(2)}, u32[]{:S(2)}) collective-permute-start(f32[100,512]{1,0:T(8,128)S(1)} %get-tuple-element.48), channel_id=1, source_target_pairs={{16,0},{0,16},{48,32},{32,48},{80,64},{64,80},{112,96},{96,112},{1... | collective-permute-start | bytes 614408 | tf_op jit(solution)/shard_map/ppermute | solution.py:404
  68.9 6.6 %collective-permute-start.12 = (f32[100,512]{1,0:T(8,128)S(1)}, f32[100,512]{1,0:T(8,128)S(1)}, u32[]{:S(2)}, u32[]{:S(2)}) collective-permute-start(f32[100,512]{1,0:T(8,128)S(1)} %join_tails.2), channel_id=1, source_target_pairs={{0,96},{32,0},{64,32},{96,64},{1,97},{33,1},{65,33},{97,65},{2,98}... | collective-permute-start | bytes 614408 | tf_op jit(solution)/shard_map/ppermute | solution.py:390
  72.4 6.2 %collective-permute-start.13 = (f32[100,512]{1,0:T(8,128)S(1)}, f32[100,512]{1,0:T(8,128)S(1)}, u32[]{:S(2)}, u32[]{:S(2)}) collective-permute-start(f32[100,512]{1,0:T(8,128)S(1)} %join_tails.3), channel_id=1, source_target_pairs={{0,32},{32,64},{64,96},{96,0},{1,33},{33,65},{65,97},{97,1},{2,34}... | collective-permute-start | bytes 614408 | tf_op jit(solution)/shard_map/ppermute | solution.py:390
  78.5 3.4 %copy-start.1 = (bf16[8,1024,512]{2,1,0:T(8,128)(2,1)S(1)}, bf16[8,1024,512]{2,1,0:T(8,128)(2,1)}, u32[]{:S(2)}) copy-start(bf16[8,1024,512]{2,1,0:T(8,128)(2,1)} %copy-done) | copy-start | bytes 25165828
  102.1 7.4 %collective-permute-start.14 = (f32[64,8,1152]{2,1,0:T(8,128)S(1)}, f32[64,8,1152]{2,1,0:T(8,128)S(1)}, u32[]{:S(2)}, u32[]{:S(2)}) collective-permute-start(f32[64,8,1152]{2,1,0:T(8,128)S(1)} %get-tuple-element.54), channel_id=1, source_target_pairs={{0,1},{1,0},{2,3},{3,2},{4,5},{5,4},{6,7},{7,6},{8,9},{9,8},{10,11... | collective-permute-start | bytes 7077896 | tf_op jit(solution)/shard_map/ppermute | solution.py:371
  111.3 41.4 %all-to-all-start = ((f32[64,8,1152]{2,1,0:T(8,128)}), f32[64,8,1152]{2,1,0:T(8,128)S(1)}, u32[]{:S(2)}, u32[]{:S(2)}) async-start(f32[64,8,1152]{2,1,0:T(8,128)} %add.50), calls=%async_computation | async-start | bytes 4718592 | tf_op jit(solution)/shard_map/all_to_all | solution.py:372
